TPU v7x, 32 devices: a whole 2x2x4 slice. The times are simulated.
32 devices in a mesh: context: 4 (over z), dp: 4 (over y, core), head: 2 (over x).
Axes of the slice: x: 2, y: 2, z: 4, core: 2. Of those that a mesh axis runs over, the one named last changes fastest.
Arguments:
- inputs: bfloat16 [4, 512, 2304], P('dp', 'context', 'head'), may hold values from -6 to 6
- output_grad: bfloat16 [4, 512, 2304], P('dp', 'context', 'head'), may hold values from -6 to 6
- qkv_weight: bfloat16 [2304, 3, 4096], P(None, None, 'head'), may hold values from -0.125 to 0.125
- out_weight: bfloat16 [2304, 4096], P(None, 'head'), may hold values from -0.09375 to 0.09375
- down_weight: bfloat16 [2304, 128], replicated, may hold values from -0.125 to 0.125
- up_weight: bfloat16 [128, 4096], P(None, 'head'), may hold values from -0.5 to 0.5
- beta_weight: bfloat16 [2304, 32], P(None, 'head'), may hold values from -0.125 to 0.125
- gate_bias: float32 [4096], P('head'), may hold values from -9 to -1.6, as said below
Outputs:
- layer_out: bfloat16 [4, 512, 2304], P('dp', 'context', 'head')
- input_grad: bfloat16 [4, 512, 2304], P('dp', 'context', 'head')
- qkv_grad: bfloat16 [2304, 3, 4096], P(('context', 'dp'), None, 'head')
- out_grad: bfloat16 [2304, 4096], P(('context', 'dp'), 'head')
- up_grad: float32 [128, 4096], P(None, 'head')
- down_grad: float32 [2304, 128], replicated
- beta_grad: float32 [2304, 32], P(None, 'head')
- bias_grad: float32 [4096], P('head')
Inputs may be any that keep to these rules, and one draw needn't show every extreme that they name: `gate_bias`: offsets of the decay gate, one per channel.
All inputs are finite; a program needn't handle non-finite values.
Results may differ from a plain program's by a relative error of at most 0.02.
Values may be sent and summed in bfloat16 or wider, within the bound.
A program may use at most 192 MiB of HBM per device.

v0:
```python
import jax
import jax.numpy as jnp
from jax import lax
from jax.sharding import PartitionSpec as P

SPAN = 64
epsilon = 1e-06
highest = lax.Precision.HIGH


def shifted(value, axis, by):
    count = lax.axis_size(axis)
    pairs = [(i, i + by) for i in range(count) if 0 <= i + by < count]
    return lax.ppermute(value, axis, pairs)


def product(pattern, left, right):
    return jnp.einsum(pattern, left, right, precision=highest)


def activate(projected, gate_pre, beta_logit):
    token_count = projected.shape[0]
    head_count = beta_logit.shape[1]
    head_width = projected.shape[2] // head_count
    blocks = projected.reshape(token_count, 3, head_count, head_width)

    def normalize(values):
        return values * lax.rsqrt(jnp.sum(values * values, axis=-1, keepdims=True) + epsilon)

    queries = jnp.swapaxes(normalize(blocks[:, 0]), 0, 1)
    key_rows = jnp.swapaxes(normalize(blocks[:, 1]), 0, 1)
    value_rows = jnp.swapaxes(blocks[:, 2], 0, 1)
    decays = jnp.swapaxes(
        (-0.25 * jax.nn.sigmoid(gate_pre)).reshape(token_count, head_count, head_width), 0, 1
    )
    betas = jnp.swapaxes(jax.nn.sigmoid(beta_logit), 0, 1)
    return (queries, key_rows, value_rows, decays, betas)


def span_terms(queries, key_rows, value_rows, decays, betas):
    leading = queries.shape[:-2]
    block_count = queries.shape[-2] // SPAN

    def blocked(member):
        return member.reshape(leading + (block_count, SPAN) + member.shape[-1:])

    queries, key_rows, value_rows, decays = (
        blocked(queries),
        blocked(key_rows),
        blocked(value_rows),
        blocked(decays),
    )
    betas = betas.reshape(leading + (block_count, SPAN))
    cumulative = jnp.cumsum(decays, axis=-2)
    middle = cumulative[..., SPAN // 2 - 1 : SPAN // 2, :]
    final_decay = cumulative[..., SPAN - 1 :, :]
    key_fwd = jnp.exp(cumulative - middle) * key_rows
    key_back = jnp.exp(middle - cumulative) * key_rows
    query_fwd = jnp.exp(cumulative - middle) * queries
    key_start = jnp.exp(cumulative) * key_rows
    query_start = jnp.exp(cumulative) * queries
    key_end = jnp.exp(final_decay - cumulative) * key_rows
    row_index = lax.broadcasted_iota(jnp.int32, (SPAN, SPAN), 0)
    col_index = lax.broadcasted_iota(jnp.int32, (SPAN, SPAN), 1)
    strict = (row_index > col_index).astype(jnp.float32)
    lower_mask = (row_index >= col_index).astype(jnp.float32)
    coupling = betas[..., :, None] * product("...tc,...sc->...ts", key_fwd, key_back) * strict
    powers = -coupling
    inverse = jnp.eye(SPAN, dtype=jnp.float32) + powers
    for section in range(1, (SPAN - 1).bit_length()):
        powers = product("...ts,...su->...tu", powers, powers)
        inverse = inverse + product("...ts,...su->...tu", inverse, powers)
    solver = inverse * betas[..., None, :]
    solved_values = product("...ts,...sc->...tc", solver, value_rows)
    solved_keys = product("...ts,...sc->...tc", solver, key_start)
    scores = product("...tc,...sc->...ts", query_fwd, key_back) * lower_mask
    query_eff = query_start - product("...ts,...sc->...tc", scores, solved_keys)
    local_out = product("...ts,...sc->...tc", scores, solved_values)
    side = queries.shape[-1]
    diagonal = jnp.eye(side, dtype=jnp.float32) * jnp.exp(final_decay)[..., 0, :, None]
    transition = diagonal - product("...sc,...sd->...cd", key_end, solved_keys)
    offset = product("...sc,...sd->...cd", key_end, solved_values)
    return (query_eff, local_out, transition, offset)


def chain(terms, state_in):

    def chain_advance(carried, pieces):
        query_eff, local_out, transition, offset = pieces
        emitted = product("...tc,...cd->...td", query_eff, carried) + local_out
        return (product("...cd,...de->...ce", transition, carried) + offset, emitted)

    moved = tuple((jnp.moveaxis(member, -3, 0) for member in terms))
    final_state, emitted = lax.scan(chain_advance, state_in, moved)
    return (jnp.moveaxis(emitted, 0, -3), final_state)


def compose_spans(transition, offset, identity):

    def compose_advance(carried, pieces):
        return (
            (
                product("hcd,hde->hce", pieces[0], carried[0]),
                product("hcd,hde->hce", pieces[0], carried[1]) + pieces[1],
            ),
            None,
        )

    moved = (jnp.moveaxis(transition, -3, 0), jnp.moveaxis(offset, -3, 0))
    combined, unused_rows = lax.scan(compose_advance, (identity, jnp.zeros_like(identity)), moved)
    return combined


def shards(
    inputs, output_grad, qkv_weight, out_weight, down_weight, up_weight, beta_weight, gate_bias
):
    gathered = lax.all_gather(inputs, "head", axis=2, tiled=True)[0]
    token_count, model_width = gathered.shape
    all_width = qkv_weight.shape[2]
    head_count = beta_weight.shape[1]
    head_width = all_width // head_count
    qkv_flat = qkv_weight.reshape(model_width, 3 * all_width)
    projected = jnp.dot(gathered, qkv_flat, preferred_element_type=jnp.float32).reshape(
        token_count, 3, all_width
    )
    low_rank = jnp.dot(gathered, down_weight, preferred_element_type=jnp.float32).astype(
        jnp.bfloat16
    )
    gate_pre = jnp.dot(low_rank, up_weight, preferred_element_type=jnp.float32) + gate_bias
    beta_logit = jnp.dot(gathered, beta_weight, preferred_element_type=jnp.float32)
    acts, act_vjp = jax.vjp(activate, projected, gate_pre, beta_logit)
    terms, terms_vjp = jax.vjp(span_terms, *acts)
    identity = jnp.broadcast_to(
        jnp.eye(head_width, dtype=jnp.float32), (head_count, head_width, head_width)
    )
    empty = jnp.zeros((head_count, head_width, head_width), jnp.float32)
    shard_linear, shard_offset = compose_spans(terms[2], terms[3], identity)
    grad_whole = lax.all_gather(output_grad, "head", axis=2, tiled=True)[0]
    mixed_grad = jnp.dot(grad_whole, out_weight, preferred_element_type=jnp.float32)
    grad_blocks = jnp.swapaxes(
        mixed_grad.reshape(token_count, head_count, head_width), 0, 1
    ).reshape(terms[1].shape)
    own_grad = jnp.zeros_like(empty)
    for block in reversed(range(token_count // SPAN)):
        own_grad = product("hcd,hce->hde", terms[2][:, block], own_grad) + product(
            "htc,htd->hcd", terms[0][:, block], grad_blocks[:, block]
        )
    linear_back = jnp.swapaxes(shard_linear, 1, 2)
    shard_count = lax.axis_size("context")
    shard_index = lax.axis_index("context")
    state_in, state_grad = (empty, empty)
    for step in range(shard_count - 1):
        leaving = shard_offset
        leaving_grad = own_grad
        if step:
            leaving = product("hcd,hde->hce", shard_linear, state_in) + leaving
            leaving_grad = product("hcd,hde->hce", linear_back, state_grad) + leaving_grad
        state_in = shifted(leaving.astype(jnp.bfloat16), "context", 1).astype(jnp.float32)
        state_grad = shifted(leaving_grad.astype(jnp.bfloat16), "context", -1).astype(jnp.float32)
    (mixed_blocks, final_state), chain_vjp = jax.vjp(chain, terms, state_in)
    mixed = jnp.swapaxes(mixed_blocks.reshape(head_count, token_count, head_width), 0, 1)
    mixed = mixed.reshape(token_count, all_width).astype(jnp.bfloat16)
    slab = model_width // shard_count

    def slab_of(member):
        whole = lax.all_gather(member, "context", axis=0, tiled=True)
        return lax.dynamic_slice_in_dim(whole, shard_index * slab, slab, axis=1)

    def weight_term(rows, columns):
        whole = lax.all_gather(columns, "context", axis=0, tiled=True)
        term = jnp.einsum("tr,tc->rc", rows, whole, preferred_element_type=jnp.float32)
        return lax.psum_scatter(term.astype(jnp.bfloat16), "dp", scatter_dimension=0, tiled=True)

    input_slab = slab_of(gathered)
    grad_slab = slab_of(grad_whole)
    out_grad = weight_term(grad_slab, mixed)
    out_part = jnp.einsum("tc,dc->td", mixed, out_weight, preferred_element_type=jnp.float32)
    layer_out = lax.psum_scatter(
        out_part.astype(jnp.bfloat16), "head", scatter_dimension=1, tiled=True
    )[None]
    term_grads, unused_state = chain_vjp((grad_blocks, state_grad))
    proj_grad, pre_grad, logit_grad = act_vjp(terms_vjp(term_grads))
    proj_parts = [proj_grad[:, part].astype(jnp.bfloat16) for part in range(3)]
    qkv_grad = jnp.stack([weight_term(input_slab, part) for part in proj_parts], axis=1)
    gate_low = pre_grad.astype(jnp.bfloat16)
    logit_low = logit_grad.astype(jnp.bfloat16)
    low_grad = jnp.einsum(
        "tc,rc->tr", gate_low, up_weight, preferred_element_type=jnp.float32
    ).astype(jnp.bfloat16)
    up_term = jnp.einsum("tr,tc->rc", low_rank, gate_low, preferred_element_type=jnp.float32)
    beta_term = jnp.einsum("td,th->dh", gathered, logit_low, preferred_element_type=jnp.float32)
    bias_term = jnp.sum(pre_grad, axis=0)
    down_term = jnp.einsum("td,tr->dr", gathered, low_grad, preferred_element_type=jnp.float32)
    small = [up_term, down_term, beta_term, bias_term]
    packed = jnp.concatenate([term.astype(jnp.bfloat16).reshape(-1, 128) for term in small], axis=0)
    packed = lax.psum(packed, ("context", "dp")).astype(jnp.float32)
    results, start = ([], 0)
    for term in small:
        count = term.size // 128
        results.append(packed[start : start + count].reshape(term.shape))
        start += count
    up_grad, down_grad, beta_grad, bias_grad = results
    down_grad = lax.psum(down_grad, "head")
    input_part = jnp.einsum("tr,dr->td", low_grad, down_weight, preferred_element_type=jnp.float32)
    input_part = input_part + jnp.einsum(
        "th,dh->td", logit_low, beta_weight, preferred_element_type=jnp.float32
    )
    input_part = input_part + jnp.einsum(
        "tc,dc->td",
        jnp.concatenate(proj_parts, axis=1),
        qkv_flat,
        preferred_element_type=jnp.float32,
    )
    input_grad = lax.psum_scatter(
        input_part.astype(jnp.bfloat16), "head", scatter_dimension=1, tiled=True
    )[None]
    return (layer_out, input_grad, qkv_grad, out_grad, up_grad, down_grad, beta_grad, bias_grad)


def solution(mesh):
    return jax.shard_map(
        shards,
        mesh=mesh,
        in_specs=(
            P("dp", "context", "head"),
            P("dp", "context", "head"),
            P(None, None, "head"),
            P(None, "head"),
            P(),
            P(None, "head"),
            P(None, "head"),
            P("head"),
        ),
        out_specs=(
            P("dp", "context", "head"),
            P("dp", "context", "head"),
            P(("context", "dp"), None, "head"),
            P(("context", "dp"), "head"),
            P(None, "head"),
            P(),
            P(None, "head"),
            P("head"),
        ),
        check_vma=False,
    )
```

profile of v0, /device:TPU:0, one launch (start us, length us, event | category | flops | bytes accessed | tf_op | source)
XLA Modules:
  0.0 760.1 jit_solution(1291417502378739657)
XLA Ops:
  8.1 11.0 %all_gather.24 = bf16[1,128,2304]{2,1,0:T(8,128)(2,1)S(1)} all-gather(bf16[1,128,1152]{2,1,0:T(8,128)(2,1)} %param.14), channel_id=1, replica_groups=mesh['context'=4,'dp'=4,'head'=2] {'head'}, dimensions={2}, use_global_device_ids=true | all-gather | bytes 884736 | tf_op jit(solution)/shard_map/all_gather | solution.py:117
  22.9 35.1 %copy.152 = bf16[2304,3,2048]{0,2,1:T(8,128)(2,1)} copy(bf16[2304,3,2048]{2,0,1:T(8,128)(2,1)} %param.16) | data formatting | bytes 56623104 | tf_op args[2]
  58.0 15.4 %fusion.134 = f32[128,3,16,128]{3,0,2,1:T(8,128)} fusion(bf16[3,16,128,2304]{3,2,1,0:T(8,128)(2,1)} %bitcast.472, bf16[1,128,2304]{2,1,0:T(8,128)(2,1)S(1)} %all_gather.24), kind=kOutput, calls=%fused_computation.216 | convolution fusion | flops 3623878656 | bytes 32047104 | tf_op jit(solution)/shard_map/dot_general | solution.py:123
  99.8 3.2 bitcast_subtract_fusion
  107.0 12.9 %while.51 = (s32[]{:T(128)}, f32[16,128,128]{2,1,0:T(8,128)}, f32[16,128,128]{2,1,0:T(8,128)}, f32[2,16,128,128]{3,2,1,0:T(8,128)}, f32[2,16,128,128]{3,2,1,0:T(8,128)}, /*index=5*/s32[]{:T(128)}, s32[]{:T(128)}) while((s32[]{:T(128)}, f32[16,128,128]{2,1,0:T(8,128)}, f32[16,128,128]{2,1,0:T(8,128)}, ...), condition=%wide.region_3.4_spmd.clone, body=%wide.region_2.0_spmd.clone.sunk | while | flops 403177472 | bytes 24118416 | solution.py:110
  122.2 4.5 collective-permute-start
  134.9 8.4 %all_gather.25 = bf16[1,128,2304]{2,1,0:T(8,128)(2,1)} all-gather(bf16[1,128,1152]{2,1,0:T(8,128)(2,1)S(1)} %copy-done.97), channel_id=1, replica_groups=mesh['context'=4,'dp'=4,'head'=2] {'head'}, dimensions={2}, use_global_device_ids=true | all-gather | bytes 884736 | tf_op jit(solution)/shard_map/all_gather | solution.py:138
  143.2 13.1 %copy.257 = bf16[2048,2304]{1,0:T(8,128)(2,1)} copy(bf16[2048,2304]{0,1:T(8,128)(2,1)} %bitcast.482) | data formatting | bytes 18874368 | tf_op jit(solution)/shard_map/dot_general | solution.py:139
  156.4 5.8 fusion.136
  172.4 5.4 collective-permute-start.1
  187.7 4.4 collective-permute-start.2
  193.7 3.5 collective-permute-done.4
  201.7 9.2 %while.49 = (s32[]{:T(128)}, f32[16,128,128]{2,1,0:T(8,128)S(1)}, bf16[2,16,64,128]{3,2,0,1:T(8,128)(2,1)}, f32[2,16,128,128]{3,2,1,0:T(8,128)}, f32[2,16,128,12...) while((s32[]{:T(128)}, f32[16,128,128]{2,1,0:T(8,128)S(1)}, ...), condition=%wide.region_6.7_spmd, body=%wide.region_5.6_spmd.sunk | while | flops 302383104 | bytes 36178636 | solution.py:94
  217.5 23.3 %while.50 = (s32[]{:T(128)}, f32[16,128,128]{2,1,0:T(8,128)S(1)}, f32[2,16,64,128]{3,2,0,1:T(8,128)}, f32[2,16,64,128]{3,2,1,0:T(8,128)}, f32[2,16,128,128]{2,3,...) while((s32[]{:T(128)}, f32[16,128,128]{2,1,0:T(8,128)S(1)}, ...), condition=%wide.region_9.10_spmd, body=%wide.region_8.9_spmd.sunk | while | flops 604241920 | bytes 56627016 | solution.py:94
  217.5 3.6 fusion.360
  229.1 3.5 fusion.360
  290.5 4.5 fusion.66
  303.5 3.8 fusion.98
  314.7 3.3 concatenate.7
  332.9 11.5 %fusion.57 = f32[128,2304]{1,0:T(8,128)S(1)} fusion(bf16[2304,6144]{0,1:T(8,128)(2,1)} %bitcast.473, bf16[128,2048]{0,1:T(8,128)(2,1)S(1)} %copy-done.93, bf16[128,2048]{0,1:T(8,128)(2,1)S(1)} %get-tuple-element.464, bf16[128,2048]{0,1:T(8,128)(2,1)S(1)} %get-tuple-element.463), kind=kOutput, calls=%fused_computation.83 | convolution fusion | flops 3628597248 | bytes 31064064 | tf_op jit(solution)/shard_map/tc,dc->td/dot_general | solution.py:208
  346.1 7.1 convolution_convert_fusion.1
  354.3 175.0 %all-reduce.8.cloned.1.call-done = bf16[4656,128]{0,1:T(8,128)(2,1)} async-done(((bf16[4656,128]{0,1:T(8,128)(2,1)}), bf16[4656,128]{0,1:T(8,128)(2,1)}) %all-reduce.8.cloned.1.call-update) | async-done | bytes 1191952 | tf_op jit(solution)/shard_map/psum | solution.py:196
  531.6 5.1 convolution_convert_fusion.6
  538.5 4.9 convolution_convert_fusion.5
  543.5 4.9 convolution_convert_fusion.4
  548.5 21.4 %all-gather.22.cloned.1.call-done = bf16[1,512,2304]{2,1,0:T(8,128)(2,1)} async-done(((bf16[1,128,2304]{2,1,0:T(8,128)(2,1)}), bf16[1,512,2304]{2,1,0:T(8,128)(2,1)}) %all-gather.22.cloned.1.call-update) | async-done | bytes 2359312 | tf_op jit(solution)/shard_map/all_gather | solution.py:166
  569.9 47.1 %all-gather.12.cloned.1.call-done = bf16[512,2048]{0,1:T(8,128)(2,1)} async-done(((bf16[128,2048]{0,1:T(8,128)(2,1)}), bf16[512,2048]{0,1:T(8,128)(2,1)}) %all-gather.12.cloned.1.call-update) | async-done | bytes 2097168 | tf_op jit(solution)/shard_map/all_gather | solution.py:170
  616.9 5.6 convolution_convert_fusion.3
  636.2 9.6 %reduce-scatter.11.cloned.1.call-done = bf16[144,2048]{1,0:T(8,128)(2,1)} async-done(((bf16[576,2048]{1,0:T(8,128)(2,1)}), bf16[144,2048]{1,0:T(8,128)(2,1)}) %reduce-scatter.11.cloned.1.call-update) | async-done | bytes 589840 | tf_op jit(solution)/shard_map/reduce_scatter | solution.py:172
  645.8 35.2 %reduce-scatter.13.cloned.1.call-done = bf16[144,2048]{1,0:T(8,128)(2,1)} async-done(((bf16[576,2048]{1,0:T(8,128)(2,1)}), bf16[144,2048]{1,0:T(8,128)(2,1)}) %reduce-scatter.13.cloned.1.call-update) | async-done | bytes 589840 | tf_op jit(solution)/shard_map/reduce_scatter | solution.py:172
  681.1 35.4 %reduce-scatter.15.cloned.1.call-done = bf16[144,2048]{1,0:T(8,128)(2,1)} async-done(((bf16[576,2048]{1,0:T(8,128)(2,1)}), bf16[144,2048]{1,0:T(8,128)(2,1)}) %reduce-scatter.15.cloned.1.call-update) | async-done | bytes 589840 | tf_op jit(solution)/shard_map/reduce_scatter | solution.py:172
  719.3 33.1 %reduce-scatter.17.cloned.1.call-done = bf16[144,2048]{1,0:T(8,128)(2,1)} async-done(((bf16[576,2048]{1,0:T(8,128)(2,1)}), bf16[144,2048]{1,0:T(8,128)(2,1)}) %reduce-scatter.17.cloned.1.call-update) | async-done | bytes 589840 | tf_op jit(solution)/shard_map/reduce_scatter | solution.py:172
  (444 shorter events, 217.7 us)
Async XLA Ops:
  8.0 11.2 %copy-start = (bf16[2304,128]{1,0:T(8,128)(2,1)S(1)}, bf16[2304,128]{1,0:T(8,128)(2,1)}, u32[]{:S(2)}) copy-start(bf16[2304,128]{1,0:T(8,128)(2,1)} %param.18) | copy-start | bytes 1769476
  8.0 11.5 %copy-start.95 = (bf16[128,2048]{1,0:T(8,128)(2,1)S(1)}, bf16[128,2048]{1,0:T(8,128)(2,1)}, u32[]{:S(2)}) copy-start(bf16[128,2048]{1,0:T(8,128)(2,1)} %param.19) | copy-start | bytes 1572868
  8.0 11.5 %copy-start.103 = (f32[2048]{0:T(1024)S(1)}, f32[2048]{0:T(1024)}, u32[]{:S(2)}) copy-start(f32[2048]{0:T(1024)} %param.21) | copy-start | bytes 24580
  8.0 521.3 %all-reduce.8.cloned.1.call-start = ((), (), s32[]{:S(2)}) async-start(), calls=%async_computation.11 | async-start | bytes 2424832 | tf_op jit(solution)/shard_map/psum | solution.py:196
  19.1 294.2 %copy-start.37 = (bf16[1,128,2304]{2,1,0:T(8,128)(2,1)}, bf16[1,128,2304]{2,1,0:T(8,128)(2,1)S(1)}, u32[]{:S(2)}) copy-start(bf16[1,128,2304]{2,1,0:T(8,128)(2,1)S(1)} %all_gather.24) | copy-start | bytes 1769476
  81.2 45.5 %copy-start.3 = (f32[128,16,128]{2,0,1:T(8,128)}, f32[128,16,128]{2,0,1:T(8,128)S(1)}, u32[]{:S(2)}) copy-start(f32[128,16,128]{2,0,1:T(8,128)S(1)} %get-tuple-element.459) | copy-start | bytes 3145732
  92.6 7.2 copy-start.46
  119.9 6.7 copy-start.33
  122.2 47.9 %collective-permute-start = (bf16[16,128,128]{2,1,0:T(8,128)(2,1)}, bf16[16,128,128]{2,1,0:T(8,128)(2,1)}, u32[]{:S(2)}, u32[]{:S(2)}) collective-permute-start(bf16[16,128,128]{2,1,0:T(8,128)(2,1)} %convert_element_type.153), channel_id=1, source_target_pairs={{0,8},{8,16},{16,24},{1,9},{9,17},{17,25},{2,10},{10,18},{18,26},{... | collective-permute-start | bytes 1572872 | tf_op jit(solution)/shard_map/ppermute | solution.py:14
  130.2 32.1 %copy-start.72 = (f32[16,2,64,128]{3,2,1,0:T(8,128)}, f32[16,2,64,128]{3,2,1,0:T(8,128)S(1)}, u32[]{:S(2)}) copy-start(f32[16,2,64,128]{3,2,1,0:T(8,128)S(1)} %convolution_subtract_fusion) | copy-start | bytes 3145732
  168.7 13.9 %collective-permute-start.3 = (bf16[16,128,128]{2,1,0:T(8,128)(2,1)}, bf16[16,128,128]{2,1,0:T(8,128)(2,1)}, u32[]{:S(2)}, u32[]{:S(2)}) collective-permute-start(bf16[16,128,128]{2,1,0:T(8,128)(2,1)} %get-tuple-element.474), channel_id=1, source_target_pairs={{8,0},{16,8},{24,16},{9,1},{17,9},{25,17},{10,2},{18,10},{26,18},{... | collective-permute-start | bytes 1572872 | tf_op jit(solution)/shard_map/ppermute | solution.py:14
  172.4 13.7 %collective-permute-start.1 = (bf16[16,128,128]{2,1,0:T(8,128)(2,1)}, bf16[16,128,128]{2,1,0:T(8,128)(2,1)}, u32[]{:S(2)}, u32[]{:S(2)}) collective-permute-start(bf16[16,128,128]{2,1,0:T(8,128)(2,1)} %fusion.77), channel_id=1, source_target_pairs={{0,8},{8,16},{16,24},{1,9},{9,17},{17,25},{2,10},{10,18},{18,26},{... | collective-permute-start | bytes 1572872 | tf_op jit(solution)/shard_map/ppermute | solution.py:14
  184.4 7.7 %copy-start.39 = (f32[16,2,64,128]{3,2,1,0:T(8,128)S(1)}, f32[16,2,64,128]{3,2,1,0:T(8,128)}, u32[]{:S(2)}) copy-start(f32[16,2,64,128]{3,2,1,0:T(8,128)} %copy-done.38) | copy-start | bytes 3145732
  184.4 7.7 %copy-start.44 = (f32[16,2,64,64]{3,2,1,0:T(8,128)S(1)}, f32[16,2,64,64]{3,2,1,0:T(8,128)}, u32[]{:S(2)}) copy-start(f32[16,2,64,64]{3,2,1,0:T(8,128)} %copy-done.43) | copy-start | bytes 1572868
  184.4 12.8 %collective-permute-start.4 = (bf16[16,128,128]{2,1,0:T(8,128)(2,1)S(1)}, bf16[16,128,128]{2,1,0:T(8,128)(2,1)S(1)}, u32[]{:S(2)}, u32[]{:S(2)}) collective-permute-start(bf16[16,128,128]{2,1,0:T(8,128)(2,1)S(1)} %fusion.79), channel_id=1, source_target_pairs={{8,0},{16,8},{24,16},{9,1},{17,9},{25,17},{10,2},{18,10},{26,18},{... | collective-permute-start | bytes 1572872 | tf_op jit(solution)/shard_map/ppermute | solution.py:14
  187.7 12.4 %collective-permute-start.2 = (bf16[16,128,128]{2,1,0:T(8,128)(2,1)S(1)}, bf16[16,128,128]{2,1,0:T(8,128)(2,1)S(1)}, u32[]{:S(2)}, u32[]{:S(2)}) collective-permute-start(bf16[16,128,128]{2,1,0:T(8,128)(2,1)S(1)} %fusion.78), channel_id=1, source_target_pairs={{0,8},{8,16},{16,24},{1,9},{9,17},{17,25},{2,10},{10,18},{18,26},{... | collective-permute-start | bytes 1572872 | tf_op jit(solution)/shard_map/ppermute | solution.py:14
  198.8 12.2 %collective-permute-start.5 = (bf16[16,128,128]{2,1,0:T(8,128)(2,1)}, bf16[16,128,128]{2,1,0:T(8,128)(2,1)}, u32[]{:S(2)}, u32[]{:S(2)}) collective-permute-start(bf16[16,128,128]{2,1,0:T(8,128)(2,1)} %fusion.80), channel_id=1, source_target_pairs={{8,0},{16,8},{24,16},{9,1},{17,9},{25,17},{10,2},{18,10},{26,18},{... | collective-permute-start | bytes 1572872 | tf_op jit(solution)/shard_map/ppermute | solution.py:14
  258.3 12.3 %copy-start.74 = (f32[16,2,64,64]{3,2,1,0:T(8,128)}, f32[16,2,64,64]{3,2,1,0:T(8,128)S(1)}, u32[]{:S(2)}) copy-start(f32[16,2,64,64]{3,2,1,0:T(8,128)S(1)} %convolution_add_fusion.7) | copy-start | bytes 1572868
  318.0 213.6 %all-gather.14.cloned.1.call-start = ((), (), s32[]{:S(2)}) async-start(), calls=%async_computation.13 | async-start | bytes 2949120 | tf_op jit(solution)/shard_map/all_gather | solution.py:166
  318.6 213.0 %all-gather.16.cloned.1.call-start = ((), (), s32[]{:S(2)}) async-start(), calls=%async_computation.14 | async-start | bytes 2621440 | tf_op jit(solution)/shard_map/all_gather | solution.py:170
  329.3 207.6 %all-gather.18.cloned.1.call-start = ((), (), s32[]{:S(2)}) async-start(), calls=%async_computation.15 | async-start | bytes 2621440 | tf_op jit(solution)/shard_map/all_gather | solution.py:170
  329.9 213.6 %all-gather.20.cloned.1.call-start = ((), (), s32[]{:S(2)}) async-start(), calls=%async_computation.16 | async-start | bytes 2621440 | tf_op jit(solution)/shard_map/all_gather | solution.py:170
  330.6 239.2 %all-gather.22.cloned.1.call-start = ((), (), s32[]{:S(2)}) async-start(), calls=%async_computation.17 | async-start | bytes 2949120 | tf_op jit(solution)/shard_map/all_gather | solution.py:166
  331.4 285.6 %all-gather.12.cloned.1.call-start = ((), (), s32[]{:S(2)}) async-start(), calls=%async_computation.9 | async-start | bytes 2621440 | tf_op jit(solution)/shard_map/all_gather | solution.py:170
  332.5 297.3 %reduce-scatter.21.cloned.1.call-start = ((), (), s32[]{:S(2)}) async-start(), calls=%async_computation.19 | async-start | bytes 884736
  332.9 11.5 %copy-start.99 = (bf16[2304,16]{0,1:T(8,128)(2,1)S(1)}, bf16[2304,16]{0,1:T(8,128)(2,1)}, u32[]{:S(2)}) copy-start(bf16[2304,16]{0,1:T(8,128)(2,1)} %param.20) | copy-start | bytes 221188
  345.8 285.9 %reduce-scatter.19.cloned.1.call-start = ((), (), s32[]{:S(2)}) async-start(), calls=%async_computation.18 | async-start | bytes 884736
  354.3 279.2 %all-reduce.10.cloned.1.call-start = ((), (), s32[]{:S(2)}) async-start(), calls=%async_computation.12 | async-start | bytes 2359296 | tf_op jit(solution)/shard_map/psum | solution.py:203
  531.5 114.3 %reduce-scatter.11.cloned.1.call-start = ((), (), s32[]{:S(2)}) async-start(), calls=%async_computation.6 | async-start | bytes 2949120 | tf_op jit(solution)/shard_map/reduce_scatter | solution.py:172
  536.8 144.3 %reduce-scatter.13.cloned.1.call-start = ((), (), s32[]{:S(2)}) async-start(), calls=%async_computation.7 | async-start | bytes 2949120 | tf_op jit(solution)/shard_map/reduce_scatter | solution.py:172
  543.4 173.1 %reduce-scatter.15.cloned.1.call-start = ((), (), s32[]{:S(2)}) async-start(), calls=%async_computation.8 | async-start | bytes 2949120 | tf_op jit(solution)/shard_map/reduce_scatter | solution.py:172
  548.4 204.0 %reduce-scatter.17.cloned.1.call-start = ((), (), s32[]{:S(2)}) async-start(), calls=%async_computation.10 | async-start | bytes 2949120 | tf_op jit(solution)/shard_map/reduce_scatter | solution.py:172
  (105 other events, 231.4 us)
Sparse Core Ops, SparseCore 0:
  318.1 211.1 all-reduce.7
  531.6 14.9 reduce-scatter.20
  549.4 15.3 reduce-scatter.18
  567.6 42.9 all-reduce.9
  612.9 32.8 reduce-scatter.10
  648.2 32.8 reduce-scatter.12
  683.6 32.8 reduce-scatter.14
  719.5 32.8 reduce-scatter.16
Sparse Core Ops, SparseCore 1:
  320.6 54.9 all-gather.13
  377.1 46.4 all-gather.15
  425.0 45.9 all-gather.17
  472.5 47.0 all-gather.19
  521.1 48.7 all-gather.21
  572.0 44.9 all-gather.11
where the time goes:
time: 768 us; the launch traced here: 760 us
  waiting for transfers between devices  365 us (48%)
  matrix products  184 us (24%)
  local copies, waits for them, and re-layouts  132 us (17%)
  other arithmetic  22.7 us (3%)
  blocking collectives  19.4 us (3%)
  starting transfers between devices  19.1 us (2%)
  between operations  17.6 us (2%)
    psum x1, waiting for transfers between devices, shards(): packed = lax.psum(packed, ('context', 'dp')).astype(jnp.float32)  175 us
    dot_general x78, matrix products, product(): return jnp.einsum(pattern, left, right, precision=highest)  120 us
    reduce_scatter x4, waiting for transfers between devices, weight_term(): lax.psum_scatter(term.astype(jnp.bfloat16), 'dp', scatter_dimension=0, ti...  113 us
    unnamed x192, local copies, waits for them, and re-layouts  65.9 us
    all_gather x4, waiting for transfers between devices, weight_term(): whole = lax.all_gather(columns, 'context', axis=0, tiled=True)  47.1 us
    all_gather x2, waiting for transfers between devices, slab_of(): whole = lax.all_gather(member, 'context', axis=0, tiled=True)  21.4 us
    dot_general x4, matrix products, weight_term(): jnp.einsum('tr,tc->rc', rows, whole, preferred_element_type=jnp.float32)  20.5 us
    ppermute x6, starting transfers between devices, shifted(): return lax.ppermute(value, axis, pairs)  18.2 us
  transfers between devices with their start and end apart: 20, of which 10 were waited for; matrix products, arithmetic and copies ran while one was open for 16% of the time, Pallas kernels for 0%

commit v1 on v0

--- a/solution.py
+++ b/solution.py
@@ -193,7 +193,7 @@
     down_term = jnp.einsum("td,tr->dr", gathered, low_grad, preferred_element_type=jnp.float32)
     small = [up_term, down_term, beta_term, bias_term]
     packed = jnp.concatenate([term.astype(jnp.bfloat16).reshape(-1, 128) for term in small], axis=0)
-    packed = lax.psum(packed, ("context", "dp")).astype(jnp.float32)
+    packed = jnp.sum(lax.all_gather(packed, ("context", "dp")), axis=0).astype(jnp.float32)
     results, start = ([], 0)
     for term in small:
         count = term.size // 128

time: 768 us -> 923 us (1.20)
  waiting for transfers between devices: 365 us -> 520 us
    psum x1 -> x0, waiting for transfers between devices: 175 us -> none  [shards(): packed = lax.psum(packed, ('context', 'dp')).astype(jnp.float32)]
    all_gather x0 -> x1, waiting for transfers between devices: none -> 95 us  [shards(): lax.all_gather(packed, ('context', 'dp'))]
    all_gather x4, waiting for transfers between devices: 47.1 us -> 137 us  [weight_term(): whole = lax.all_gather(columns, 'context', axis=0, tiled=True)]
    psum x1, waiting for transfers between devices: 0.01 us -> 45.7 us  [shards(): down_grad = lax.psum(down_grad, 'head')]
    ppermute x6, waiting for transfers between devices: 5.3 us -> 41.2 us  [shifted(): return lax.ppermute(value, axis, pairs)]
    all_gather x2, waiting for transfers between devices: 21.4 us -> 44.6 us  [slab_of(): whole = lax.all_gather(member, 'context', axis=0, tiled=True)]
    unnamed x16, waiting for transfers between devices: 2.58 us -> 24.4 us
    reduce_scatter x4, waiting for transfers between devices: 113 us -> 132 us  [weight_term(): lax.psum_scatter(term.astype(jnp.bfloat16), 'dp', scatter_dimension=0, ti...]
  transfers between devices with their start and end apart: 20 -> 20, of which waited for: 10 -> 17; matrix products, arithmetic and copies ran while one was open for 16% -> 24% of each run, Pallas kernels for 0% -> 0%
where the time goes in v1:
time: 923 us; the launch traced here: 915 us
  waiting for transfers between devices  520 us (56%)
  matrix products  182 us (20%)
  local copies, waits for them, and re-layouts  127 us (14%)
  other arithmetic  31.8 us (3%)
  starting transfers between devices  19.3 us (2%)
  blocking collectives  19.3 us (2%)
  between operations  16 us (2%)
    all_gather x4, waiting for transfers between devices, weight_term(): whole = lax.all_gather(columns, 'context', axis=0, tiled=True)  137 us
    reduce_scatter x4, waiting for transfers between devices, weight_term(): lax.psum_scatter(term.astype(jnp.bfloat16), 'dp', scatter_dimension=0, ti...  132 us
    dot_general x78, matrix products, product(): return jnp.einsum(pattern, left, right, precision=highest)  119 us
    all_gather x1, waiting for transfers between devices, shards(): lax.all_gather(packed, ('context', 'dp'))  95 us
    unnamed x196, local copies, waits for them, and re-layouts  61.7 us
    psum x1, waiting for transfers between devices, shards(): down_grad = lax.psum(down_grad, 'head')  45.7 us
    all_gather x2, waiting for transfers between devices, slab_of(): whole = lax.all_gather(member, 'context', axis=0, tiled=True)  44.6 us
    ppermute x6, waiting for transfers between devices, shifted(): return lax.ppermute(value, axis, pairs)  41.2 us
  transfers between devices with their start and end apart: 20, of which 17 were waited for; matrix products, arithmetic and copies ran while one was open for 24% of the time, Pallas kernels for 0%

profile of v1, /device:TPU:0, one launch (start us, length us, event | category | flops | bytes accessed | tf_op | source)
XLA Modules:
  0.0 915.4 jit_solution(2567976029094044964)
XLA Ops:
  7.3 11.0 %all_gather.30 = bf16[1,128,2304]{2,1,0:T(8,128)(2,1)S(1)} all-gather(bf16[1,128,1152]{2,1,0:T(8,128)(2,1)} %param.14), channel_id=1, replica_groups=mesh['context'=4,'dp'=4,'head'=2] {'head'}, dimensions={2}, use_global_device_ids=true | all-gather | bytes 884736 | tf_op jit(solution)/shard_map/all_gather | solution.py:117
  22.0 34.0 %copy.148 = bf16[2304,3,2048]{0,2,1:T(8,128)(2,1)} copy(bf16[2304,3,2048]{2,0,1:T(8,128)(2,1)} %param.16) | data formatting | bytes 56623104 | tf_op args[2]
  56.0 15.4 %fusion.134 = f32[128,3,16,128]{3,0,2,1:T(8,128)} fusion(bf16[3,16,128,2304]{3,2,1,0:T(8,128)(2,1)} %bitcast.474, bf16[1,128,2304]{2,1,0:T(8,128)(2,1)S(1)} %all_gather.30), kind=kOutput, calls=%fused_computation.216 | convolution fusion | flops 3623878656 | bytes 32047104 | tf_op jit(solution)/shard_map/dot_general | solution.py:123
  105.0 12.9 %while.51 = (s32[]{:T(128)}, f32[16,128,128]{2,1,0:T(8,128)}, f32[16,128,128]{2,1,0:T(8,128)}, f32[2,16,128,128]{3,2,1,0:T(8,128)}, f32[2,16,128,128]{3,2,1,0:T(8,128)}, /*index=5*/s32[]{:T(128)}, s32[]{:T(128)}) while((s32[]{:T(128)}, f32[16,128,128]{2,1,0:T(8,128)}, f32[16,128,128]{2,1,0:T(8,128)}, ...), condition=%wide.region_3.4_spmd.clone, body=%wide.region_2.0_spmd.clone.sunk | while | flops 403177472 | bytes 24118416 | solution.py:110
  132.9 8.3 all_gather.31
  141.2 13.1 %copy.250 = bf16[2048,2304]{1,0:T(8,128)(2,1)} copy(bf16[2048,2304]{0,1:T(8,128)(2,1)} %bitcast.484) | data formatting | bytes 18874368 | tf_op jit(solution)/shard_map/dot_general | solution.py:139
  154.3 5.6 fusion.136
  170.1 5.4 collective-permute-start.1
  192.2 30.7 %collective-permute-done.4 = bf16[16,128,128]{2,1,0:T(8,128)(2,1)S(1)} collective-permute-done((bf16[16,128,128]{2,1,0:T(8,128)(2,1)S(1)}, bf16[16,128,128]{2,1,0:T(8,128)(2,1)S(1)}, u32[]{:S(2)}, u32[]{:S(2)}) %collective-permute-start.4) | collective-permute-done | bytes 524320 | tf_op jit(solution)/shard_map/ppermute | solution.py:14
  227.4 9.6 %while.49 = (s32[]{:T(128)}, f32[16,128,128]{2,1,0:T(8,128)S(1)}, bf16[2,16,64,128]{3,2,0,1:T(8,128)(2,1)S(1)}, f32[2,16,128,128]{3,2,1,0:T(8,128)}, f32[2,16,12...) while((s32[]{:T(128)}, f32[16,128,128]{2,1,0:T(8,128)S(1)}, ...), condition=%wide.region_6.7_spmd, body=%wide.region_5.6_spmd.sunk | while | flops 302383104 | bytes 36178636 | solution.py:94
  237.1 7.2 collective-permute-done.5
  250.8 23.3 %while.50 = (s32[]{:T(128)}, f32[16,128,128]{2,1,0:T(8,128)S(1)}, f32[2,16,64,128]{3,2,0,1:T(8,128)}, f32[2,16,64,128]{3,2,1,0:T(8,128)}, f32[2,16,128,128]{2,3,...) while((s32[]{:T(128)}, f32[16,128,128]{2,1,0:T(8,128)S(1)}, ...), condition=%wide.region_9.10_spmd, body=%wide.region_8.9_spmd.sunk | while | flops 604241920 | bytes 56627016 | solution.py:94
  364.1 11.5 %fusion.57 = f32[128,2304]{1,0:T(8,128)S(1)} fusion(bf16[2304,6144]{0,1:T(8,128)(2,1)} %bitcast.475, bf16[128,2048]{0,1:T(8,128)(2,1)S(1)} %copy-done.93, bf16[128,2048]{0,1:T(8,128)(2,1)S(1)} %copy-done.92, bf16[128,2048]{0,1:T(8,128)(2,1)S(1)} %get-tuple-element.455), kind=kOutput, calls=%fused_computation.83 | convolution fusion | flops 3628597248 | bytes 31064064 | tf_op jit(solution)/shard_map/tc,dc->td/dot_general | solution.py:208
  377.1 7.0 convolution_convert_fusion.1
  385.3 8.6 all-gather.18.cloned.1.call-done
  393.9 5.1 convolution_convert_fusion.6
  399.3 40.6 %all-gather.20.cloned.1.call-done = bf16[512,1,2048]{0,2,1:T(8,128)(2,1)} async-done(((bf16[128,1,2048]{0,2,1:T(8,128)(2,1)}), bf16[512,1,2048]{0,2,1:T(8,128)(2,1)}) %all-gather.20.cloned.1.call-update) | async-done | bytes 2097168 | tf_op jit(solution)/shard_map/all_gather | solution.py:170
  439.9 4.8 convolution_convert_fusion.5
  444.8 41.0 %all-gather.22.cloned.1.call-done = bf16[512,1,2048]{0,2,1:T(8,128)(2,1)} async-done(((bf16[128,1,2048]{0,2,1:T(8,128)(2,1)}), bf16[512,1,2048]{0,2,1:T(8,128)(2,1)}) %all-gather.22.cloned.1.call-update) | async-done | bytes 2097168 | tf_op jit(solution)/shard_map/all_gather | solution.py:170
  485.8 4.9 convolution_convert_fusion.4
  490.8 44.6 %all-gather.24.cloned.1.call-done = bf16[1,512,2304]{2,1,0:T(8,128)(2,1)} async-done(((bf16[1,128,2304]{2,1,0:T(8,128)(2,1)}), bf16[1,512,2304]{2,1,0:T(8,128)(2,1)}) %all-gather.24.cloned.1.call-update) | async-done | bytes 2359312 | tf_op jit(solution)/shard_map/all_gather | solution.py:166
  535.4 47.0 %all-gather.14.cloned.1.call-done = bf16[512,2048]{0,1:T(8,128)(2,1)} async-done(((bf16[128,2048]{0,1:T(8,128)(2,1)}), bf16[512,2048]{0,1:T(8,128)(2,1)}) %all-gather.14.cloned.1.call-update) | async-done | bytes 2097168 | tf_op jit(solution)/shard_map/all_gather | solution.py:170
  582.5 5.1 convolution_convert_fusion.3
  587.7 95.0 %all-gather.26.cloned.1.call-done = bf16[74496,128]{1,0:T(8,128)(2,1)} async-done(((bf16[4656,128]{1,0:T(8,128)(2,1)}), bf16[74496,128]{1,0:T(8,128)(2,1)}) %all-gather.26.cloned.1.call-update) | async-done | bytes 19070992 | tf_op jit(solution)/shard_map/all_gather | solution.py:196
  682.7 10.5 %reduce_sum.155 = bf16[4656,128]{1,0:T(8,128)(2,1)S(1)} reduce(bf16[16,4656,128]{2,1,0:T(8,128)(2,1)} %bitcast.490, bf16[]{:T(256)} %constant.94.clone.1), dimensions={0}, to_apply=%region_26.27 | reduce | flops 8939520 | bytes 20262914 | tf_op jit(solution)/shard_map/reduce_sum | solution.py:196
  694.2 6.0 reduce-scatter.21.cloned.1.call-done
  702.1 16.4 %reduce-scatter.19.cloned.1.call-done = bf16[1152,128]{1,0:T(8,128)(2,1)} async-done(((bf16[2304,128]{1,0:T(8,128)(2,1)}), bf16[1152,128]{1,0:T(8,128)(2,1)}) %reduce-scatter.19.cloned.1.call-update) | async-done | bytes 294928
  720.4 33.4 %reduce-scatter.11.cloned.1.call-done = bf16[144,2048]{1,0:T(8,128)(2,1)} async-done(((bf16[576,2048]{1,0:T(8,128)(2,1)}), bf16[144,2048]{1,0:T(8,128)(2,1)}) %reduce-scatter.11.cloned.1.call-update) | async-done | bytes 589840 | tf_op jit(solution)/shard_map/reduce_scatter | solution.py:172
  753.7 35.4 %reduce-scatter.13.cloned.1.call-done = bf16[144,2048]{1,0:T(8,128)(2,1)} async-done(((bf16[576,2048]{1,0:T(8,128)(2,1)}), bf16[144,2048]{1,0:T(8,128)(2,1)}) %reduce-scatter.13.cloned.1.call-update) | async-done | bytes 589840 | tf_op jit(solution)/shard_map/reduce_scatter | solution.py:172
  789.1 35.2 %reduce-scatter.15.cloned.1.call-done = bf16[144,2048]{1,0:T(8,128)(2,1)} async-done(((bf16[576,2048]{1,0:T(8,128)(2,1)}), bf16[144,2048]{1,0:T(8,128)(2,1)}) %reduce-scatter.15.cloned.1.call-update) | async-done | bytes 589840 | tf_op jit(solution)/shard_map/reduce_scatter | solution.py:172
  832.6 27.7 %reduce-scatter.17.cloned.1.call-done = bf16[144,2048]{1,0:T(8,128)(2,1)} async-done(((bf16[576,2048]{1,0:T(8,128)(2,1)}), bf16[144,2048]{1,0:T(8,128)(2,1)}) %reduce-scatter.17.cloned.1.call-update) | async-done | bytes 589840 | tf_op jit(solution)/shard_map/reduce_scatter | solution.py:172
  860.3 45.7 %all-reduce.7.cloned.1.call-done = f32[2304,128]{1,0:T(8,128)} async-done(((f32[2304,128]{1,0:T(8,128)}), f32[2304,128]{1,0:T(8,128)}) %all-reduce.7.cloned.1.call-update) | async-done | bytes 1179664 | tf_op jit(solution)/shard_map/psum | solution.py:203
  (448 shorter events, 242.8 us)
Async XLA Ops:
  7.2 11.2 %copy-start = (bf16[2304,128]{1,0:T(8,128)(2,1)S(1)}, bf16[2304,128]{1,0:T(8,128)(2,1)}, u32[]{:S(2)}) copy-start(bf16[2304,128]{1,0:T(8,128)(2,1)} %param.18) | copy-start | bytes 1769476
  7.2 11.5 %copy-start.96 = (bf16[128,2048]{1,0:T(8,128)(2,1)S(1)}, bf16[128,2048]{1,0:T(8,128)(2,1)}, u32[]{:S(2)}) copy-start(bf16[128,2048]{1,0:T(8,128)(2,1)} %param.19) | copy-start | bytes 1572868
  7.2 11.5 %copy-start.105 = (f32[2048]{0:T(1024)S(1)}, f32[2048]{0:T(1024)}, u32[]{:S(2)}) copy-start(f32[2048]{0:T(1024)} %param.21) | copy-start | bytes 24580
  7.2 378.1 %all-gather.16.cloned.1.call-start = ((), (), s32[]{:S(2)}) async-start(), calls=%async_computation.12 | async-start | bytes 2949120 | tf_op jit(solution)/shard_map/all_gather | solution.py:166
  18.3 57.6 %copy-start.36 = (bf16[1,128,2304]{2,1,0:T(8,128)(2,1)}, bf16[1,128,2304]{2,1,0:T(8,128)(2,1)S(1)}, u32[]{:S(2)}) copy-start(bf16[1,128,2304]{2,1,0:T(8,128)(2,1)S(1)} %all_gather.30) | copy-start | bytes 1769476
  79.1 45.5 %copy-start.3 = (f32[128,16,128]{2,0,1:T(8,128)}, f32[128,16,128]{2,0,1:T(8,128)S(1)}, u32[]{:S(2)}) copy-start(f32[128,16,128]{2,0,1:T(8,128)S(1)} %get-tuple-element.451) | copy-start | bytes 3145732
  120.2 47.6 %collective-permute-start = (bf16[16,128,128]{2,1,0:T(8,128)(2,1)}, bf16[16,128,128]{2,1,0:T(8,128)(2,1)}, u32[]{:S(2)}, u32[]{:S(2)}) collective-permute-start(bf16[16,128,128]{2,1,0:T(8,128)(2,1)} %convert_element_type.155), channel_id=1, source_target_pairs={{0,8},{8,16},{16,24},{1,9},{9,17},{17,25},{2,10},{10,18},{18,26},{... | collective-permute-start | bytes 1572872 | tf_op jit(solution)/shard_map/ppermute | solution.py:14
  128.2 31.8 %copy-start.72 = (f32[16,2,64,128]{3,2,1,0:T(8,128)}, f32[16,2,64,128]{3,2,1,0:T(8,128)S(1)}, u32[]{:S(2)}) copy-start(f32[16,2,64,128]{3,2,1,0:T(8,128)S(1)} %convolution_subtract_fusion) | copy-start | bytes 3145732
  141.1 13.1 %copy-start.83 = (bf16[1,128,2304]{2,1,0:T(8,128)(2,1)}, bf16[1,128,2304]{2,1,0:T(8,128)(2,1)S(1)}, u32[]{:S(2)}) copy-start(bf16[1,128,2304]{2,1,0:T(8,128)(2,1)S(1)} %all_gather.31) | copy-start | bytes 1769476
  166.5 13.9 %collective-permute-start.3 = (bf16[16,128,128]{2,1,0:T(8,128)(2,1)}, bf16[16,128,128]{2,1,0:T(8,128)(2,1)}, u32[]{:S(2)}, u32[]{:S(2)}) collective-permute-start(bf16[16,128,128]{2,1,0:T(8,128)(2,1)} %get-tuple-element.466), channel_id=1, source_target_pairs={{8,0},{16,8},{24,16},{9,1},{17,9},{25,17},{10,2},{18,10},{26,18},{... | collective-permute-start | bytes 1572872 | tf_op jit(solution)/shard_map/ppermute | solution.py:14
  170.1 14.4 %collective-permute-start.1 = (bf16[16,128,128]{2,1,0:T(8,128)(2,1)}, bf16[16,128,128]{2,1,0:T(8,128)(2,1)}, u32[]{:S(2)}, u32[]{:S(2)}) collective-permute-start(bf16[16,128,128]{2,1,0:T(8,128)(2,1)} %fusion.77), channel_id=1, source_target_pairs={{0,8},{8,16},{16,24},{1,9},{9,17},{17,25},{2,10},{10,18},{18,26},{... | collective-permute-start | bytes 1572872 | tf_op jit(solution)/shard_map/ppermute | solution.py:14
  175.5 218.3 %all-gather.18.cloned.1.call-start = ((), (), s32[]{:S(2)}) async-start(), calls=%async_computation.13 | async-start | bytes 2621440 | tf_op jit(solution)/shard_map/all_gather | solution.py:170
  182.1 8.4 copy-start.39
  182.2 40.8 %collective-permute-start.4 = (bf16[16,128,128]{2,1,0:T(8,128)(2,1)S(1)}, bf16[16,128,128]{2,1,0:T(8,128)(2,1)S(1)}, u32[]{:S(2)}, u32[]{:S(2)}) collective-permute-start(bf16[16,128,128]{2,1,0:T(8,128)(2,1)S(1)} %fusion.79), channel_id=1, source_target_pairs={{8,0},{16,8},{24,16},{9,1},{17,9},{25,17},{10,2},{18,10},{26,18},{... | collective-permute-start | bytes 1572872 | tf_op jit(solution)/shard_map/ppermute | solution.py:14
  186.1 39.6 %collective-permute-start.2 = (bf16[16,128,128]{2,1,0:T(8,128)(2,1)S(1)}, bf16[16,128,128]{2,1,0:T(8,128)(2,1)S(1)}, u32[]{:S(2)}, u32[]{:S(2)}) collective-permute-start(bf16[16,128,128]{2,1,0:T(8,128)(2,1)S(1)} %fusion.78), channel_id=1, source_target_pairs={{0,8},{8,16},{16,24},{1,9},{9,17},{17,25},{2,10},{10,18},{18,26},{... | collective-permute-start | bytes 1572872 | tf_op jit(solution)/shard_map/ppermute | solution.py:14
  224.5 19.8 %collective-permute-start.5 = (bf16[16,128,128]{2,1,0:T(8,128)(2,1)}, bf16[16,128,128]{2,1,0:T(8,128)(2,1)}, u32[]{:S(2)}, u32[]{:S(2)}) collective-permute-start(bf16[16,128,128]{2,1,0:T(8,128)(2,1)} %fusion.80), channel_id=1, source_target_pairs={{8,0},{16,8},{24,16},{9,1},{17,9},{25,17},{10,2},{18,10},{26,18},{... | collective-permute-start | bytes 1572872 | tf_op jit(solution)/shard_map/ppermute | solution.py:14
  237.1 11.5 %copy-start.94 = (bf16[2,16,64,128]{3,2,0,1:T(8,128)(2,1)}, bf16[2,16,64,128]{3,2,0,1:T(8,128)(2,1)S(1)}, u32[]{:S(2)}) copy-start(bf16[2,16,64,128]{3,2,0,1:T(8,128)(2,1)S(1)} %get-tuple-element.282) | copy-start | bytes 1572868
  291.6 12.3 %copy-start.74 = (f32[16,2,64,64]{3,2,1,0:T(8,128)}, f32[16,2,64,64]{3,2,1,0:T(8,128)S(1)}, u32[]{:S(2)}) copy-start(f32[16,2,64,64]{3,2,1,0:T(8,128)S(1)} %convolution_add_fusion.7) | copy-start | bytes 1572868
  349.0 90.9 %all-gather.20.cloned.1.call-start = ((), (), s32[]{:S(2)}) async-start(), calls=%async_computation.14 | async-start | bytes 2621440 | tf_op jit(solution)/shard_map/all_gather | solution.py:170
  349.8 136.0 %all-gather.22.cloned.1.call-start = ((), (), s32[]{:S(2)}) async-start(), calls=%async_computation.15 | async-start | bytes 2621440 | tf_op jit(solution)/shard_map/all_gather | solution.py:170
  350.4 185.1 %all-gather.24.cloned.1.call-start = ((), (), s32[]{:S(2)}) async-start(), calls=%async_computation.16 | async-start | bytes 2949120 | tf_op jit(solution)/shard_map/all_gather | solution.py:166
  350.9 231.5 %all-gather.14.cloned.1.call-start = ((), (), s32[]{:S(2)}) async-start(), calls=%async_computation.9 | async-start | bytes 2621440 | tf_op jit(solution)/shard_map/all_gather | solution.py:170
  352.2 330.4 %all-gather.26.cloned.1.call-start = ((), (), s32[]{:S(2)}) async-start(), calls=%async_computation.17 | async-start | bytes 20262912 | tf_op jit(solution)/shard_map/all_gather | solution.py:196
  362.9 337.4 %reduce-scatter.21.cloned.1.call-start = ((), (), s32[]{:S(2)}) async-start(), calls=%async_computation.19 | async-start | bytes 884736
  364.1 11.5 %copy-start.99 = (bf16[2304,16]{0,1:T(8,128)(2,1)S(1)}, bf16[2304,16]{0,1:T(8,128)(2,1)}, u32[]{:S(2)}) copy-start(bf16[2304,16]{0,1:T(8,128)(2,1)} %param.20) | copy-start | bytes 221188
  377.1 341.5 %reduce-scatter.19.cloned.1.call-start = ((), (), s32[]{:S(2)}) async-start(), calls=%async_computation.18 | async-start | bytes 884736
  385.2 368.5 %reduce-scatter.11.cloned.1.call-start = ((), (), s32[]{:S(2)}) async-start(), calls=%async_computation.6 | async-start | bytes 2949120 | tf_op jit(solution)/shard_map/reduce_scatter | solution.py:172
  399.0 40.9 %copy-start.104 = (bf16[1,512,2304]{2,1,0:T(8,128)(2,1)S(1)}, bf16[1,512,2304]{2,1,0:T(8,128)(2,1)}, u32[]{:S(2)}) copy-start(bf16[1,512,2304]{2,1,0:T(8,128)(2,1)} %all-gather.16.cloned.1.call-done) | copy-start | bytes 7077892
  399.0 390.1 %reduce-scatter.13.cloned.1.call-start = ((), (), s32[]{:S(2)}) async-start(), calls=%async_computation.7 | async-start | bytes 2949120 | tf_op jit(solution)/shard_map/reduce_scatter | solution.py:172
  444.8 379.6 %reduce-scatter.15.cloned.1.call-start = ((), (), s32[]{:S(2)}) async-start(), calls=%async_computation.8 | async-start | bytes 2949120 | tf_op jit(solution)/shard_map/reduce_scatter | solution.py:172
  490.8 369.5 %reduce-scatter.17.cloned.1.call-start = ((), (), s32[]{:S(2)}) async-start(), calls=%async_computation.10 | async-start | bytes 2949120 | tf_op jit(solution)/shard_map/reduce_scatter | solution.py:172
  587.6 318.4 %all-reduce.7.cloned.1.call-start = ((), (), s32[]{:S(2)}) async-start(), calls=%async_computation.11 | async-start | bytes 2359296 | tf_op jit(solution)/shard_map/psum | solution.py:203
  (107 other events, 251.8 us)
Sparse Core Ops, SparseCore 0:
  175.6 63.9 all-gather.15
  349.2 44.6 all-gather.17
  395.4 44.4 all-gather.19
  441.3 44.4 all-gather.21
  487.2 48.1 all-gather.23
  537.4 45.0 all-gather.13
  584.6 97.9 all-gather.25
  684.9 15.3 reduce-scatter.20
  703.1 15.3 reduce-scatter.18
  720.9 32.7 reduce-scatter.10
  756.3 32.8 reduce-scatter.12
  791.5 32.8 reduce-scatter.14
  827.5 32.8 reduce-scatter.16
  863.0 42.9 all-reduce.6
